TPU v7x, 32 devices: a whole 2x2x4 slice. The times are simulated.
32 devices in a mesh: groups: 2 (over y), ulysses: 8 (over z, x), seq: 2 (over core).
Axes of the slice: x: 2, y: 2, z: 4, core: 2. Of those that a mesh axis runs over, the one named last changes fastest.
Arguments:
- query_states: bfloat16 [2048, 8192], P(('groups', 'ulysses', 'seq')), parts along dimension 0, may hold values from -6 to 6
- key_states: bfloat16 [2048, 1024], P(('groups', 'ulysses', 'seq')), parts along dimension 0, may hold values from -6 to 6
- value_states: bfloat16 [2048, 1024], P(('groups', 'ulysses', 'seq')), parts along dimension 0, may hold values from -6 to 6
- turn_ids: int32 [2048], P('groups'), parts along dimension 0, may hold values from 0 to 3, never falling along the last dimension, each value on 1 to 512 neighbouring positions
- judge_positions: int32 [256], P('groups'), parts along dimension 0, may hold values from 0 to 1023, as said below
Outputs:
- attended_states: bfloat16 [2048, 8192], P(('groups', 'ulysses', 'seq')), parts along dimension 0
There are 2 independent parts, one for each index of `groups`. A program takes and returns all parts, laid end to end along the dimension named above; each array names one. Nothing has to cross between parts.
Inputs may be any that keep to these rules, and one draw needn't show every extreme that they name: `turn_ids`: turn numbers never fall along the conversation; every turn spans 1 to 512 tokens, one exactly that many. `judge_positions`: distinct positions, 0 and 1023 among them.
All inputs are finite; a program needn't handle non-finite values.
Results may differ from a plain program's by a relative error of at most 0.004.
Values may be sent and summed in bfloat16 or wider, within the bound.
No kernel may reach another device: no remote copies, remote signals or barrier semaphores. Data moves between devices by JAX's collectives and lax.ppermute only.
A program may use at most 64 MiB of HBM per device.

v0:
```python
import math
import jax
import jax.numpy as jnp
from jax import lax
from jax.sharding import PartitionSpec as P

HEAD_DIM = 128
floor_score = -1e30


def absorb(
    carried,
    query_block,
    query_place,
    query_turn,
    keys_block,
    values_block,
    keys_place,
    keys_turn,
    keys_judge,
    scaling,
):
    maxima, totals, running = carried
    scores = (
        jnp.einsum("qhd,kd->qhk", query_block, keys_block, preferred_element_type=jnp.float32)
        * scaling
    )
    visible = (keys_place[None, :] <= query_place[:, None]) & (
        (keys_turn[None, :] == query_turn[:, None]) | keys_judge[None, :]
    )
    scores = jnp.where(visible[:, None, :], scores, floor_score)
    newest = jnp.maximum(maxima, jnp.max(scores, axis=2))
    factor = jnp.exp(maxima - newest)
    weights = jnp.exp(scores - newest[:, :, None])
    totals = totals * factor + jnp.sum(weights, axis=2)
    running = running * factor[:, :, None] + jnp.einsum(
        "qhk,kd->qhd",
        weights.astype(jnp.bfloat16),
        values_block,
        preferred_element_type=jnp.float32,
    )
    return (newest, totals, running)


def attend(
    carried,
    queries,
    query_place,
    query_turn,
    key_rows,
    value_rows,
    keys_place,
    keys_turn,
    keys_judge,
    scaling,
):
    query_count = queries.shape[0]
    key_count = key_rows.shape[0]
    query_step = math.gcd(query_count, 512)
    key_step = math.gcd(key_count, 512)

    def over_queries(row_index, totals_all):
        offset = row_index * query_step
        query_block = lax.dynamic_slice_in_dim(queries, offset, query_step, 0)
        block_place = lax.dynamic_slice_in_dim(query_place, offset, query_step, 0)
        block_turn = lax.dynamic_slice_in_dim(query_turn, offset, query_step, 0)
        window = tuple(
            (lax.dynamic_slice_in_dim(member, offset, query_step, 0) for member in totals_all)
        )

        def over_keys(key_index, current):
            key_offset = key_index * key_step
            keys_block = lax.dynamic_slice_in_dim(key_rows, key_offset, key_step, 0)
            values_block = lax.dynamic_slice_in_dim(value_rows, key_offset, key_step, 0)
            block_keys_place = lax.dynamic_slice_in_dim(keys_place, key_offset, key_step, 0)
            block_keys_turn = lax.dynamic_slice_in_dim(keys_turn, key_offset, key_step, 0)
            block_keys_judge = lax.dynamic_slice_in_dim(keys_judge, key_offset, key_step, 0)
            return lax.cond(
                jnp.max(block_place) >= jnp.min(block_keys_place),
                lambda inside: absorb(
                    inside,
                    query_block,
                    block_place,
                    block_turn,
                    keys_block,
                    values_block,
                    block_keys_place,
                    block_keys_turn,
                    block_keys_judge,
                    scaling,
                ),
                lambda inside: inside,
                current,
            )

        window = lax.fori_loop(0, key_count // key_step, over_keys, window)
        return tuple(
            (
                lax.dynamic_update_slice_in_dim(member, updated, offset, 0)
                for member, updated in zip(totals_all, window)
            )
        )

    return lax.fori_loop(0, query_count // query_step, over_queries, carried)


def spread(array, copies):
    row_count = array.shape[0]
    shared_heads = array.shape[1] // HEAD_DIM
    widened = jnp.broadcast_to(
        array.reshape(row_count, shared_heads, 1, HEAD_DIM),
        (row_count, shared_heads, copies // shared_heads, HEAD_DIM),
    )
    return widened.reshape(row_count, copies, HEAD_DIM)


def shards(query_states, key_states, value_states, turn_ids, judge_positions):
    tokens_here = query_states.shape[0]
    ulysses_count = lax.axis_size("ulysses")
    stripe_count = lax.axis_size("seq")
    stripe = lax.axis_index("seq")
    heads_here = query_states.shape[1] // HEAD_DIM // ulysses_count
    seq_total = tokens_here * ulysses_count * stripe_count
    scaling = 1.0 / math.sqrt(HEAD_DIM)
    positions = jnp.arange(seq_total, dtype=jnp.int32)
    judged = jnp.any(positions[:, None] == judge_positions[None, :], axis=1)
    exchanged = lax.all_to_all(
        query_states.reshape(tokens_here, ulysses_count, heads_here * HEAD_DIM),
        "ulysses",
        split_axis=1,
        concat_axis=0,
        tiled=True,
    )
    query_total = ulysses_count * tokens_here
    queries = exchanged.reshape(query_total, heads_here, HEAD_DIM)
    local_rows = jnp.arange(query_total, dtype=jnp.int32)
    query_place = (
        local_rows // tokens_here * stripe_count + stripe
    ) * tokens_here + local_rows % tokens_here
    query_turn = jnp.take(turn_ids, query_place)
    carried = (
        jnp.full((query_total, heads_here), floor_score, jnp.float32),
        jnp.zeros((query_total, heads_here), jnp.float32),
        jnp.zeros((query_total, heads_here, HEAD_DIM), jnp.float32),
    )
    keys_out, values_out = (
        lax.all_to_all(
            spread(key_states, ulysses_count), "ulysses", split_axis=1, concat_axis=0, tiled=True
        ),
        lax.all_to_all(
            spread(value_states, ulysses_count), "ulysses", split_axis=1, concat_axis=0, tiled=True
        ),
    )
    key_rows = keys_out.reshape(query_total, HEAD_DIM)
    value_rows = values_out.reshape(query_total, HEAD_DIM)
    pieces = (
        lax.all_gather(key_rows, "seq", axis=0, tiled=True),
        lax.all_gather(value_rows, "seq", axis=0, tiled=True),
    )
    piece_rows = pieces[0].shape[0]
    gathered_rows = jnp.arange(piece_rows, dtype=jnp.int32)
    source_stripe = gathered_rows // query_total
    within = gathered_rows % query_total
    key_place = (
        within // tokens_here * stripe_count + source_stripe
    ) * tokens_here + within % tokens_here
    maxima, totals, running = attend(
        carried,
        queries,
        query_place,
        query_turn,
        pieces[0],
        pieces[1],
        key_place,
        jnp.take(turn_ids, key_place),
        jnp.take(judged, key_place),
        scaling,
    )
    result = (
        (running / totals[:, :, None])
        .astype(jnp.bfloat16)
        .reshape(query_total, 1, heads_here * HEAD_DIM)
    )
    returned = lax.all_to_all(result, "ulysses", split_axis=0, concat_axis=1, tiled=True)
    return returned.reshape(tokens_here, ulysses_count * heads_here * HEAD_DIM)


def solution(mesh):
    placed = (
        P(("groups", "ulysses", "seq"), None),
        P(("groups", "ulysses", "seq"), None),
        P(("groups", "ulysses", "seq"), None),
        P("groups"),
        P("groups"),
    )
    return jax.shard_map(
        shards,
        mesh=mesh,
        in_specs=placed,
        out_specs=P(("groups", "ulysses", "seq"), None),
        check_vma=False,
    )
```

profile of v0, /device:TPU:0, one launch (start us, length us, event | category | flops | bytes accessed | tf_op | source)
XLA Modules:
  0.0 126.2 jit_solution(8405274671733121284)
XLA Ops:
  1.6 7.3 %all-to-all-start = ((bf16[64,8,128]{2,0,1:T(8,128)(2,1)}), bf16[64,8,128]{2,0,1:T(8,128)(2,1)S(1)}, u32[]{:S(2)}, u32[]{:S(2)}) async-start(bf16[64,8,128]{2,0,1:T(8,128)(2,1)} %copy_bitcast_fusion.2), calls=%async_computation | async-start | bytes 262144 | tf_op jit(solution)/shard_map/all_to_all | solution.py:147
  10.4 5.8 %all-to-all-done = bf16[64,8,128]{2,0,1:T(8,128)(2,1)S(1)} async-done(((bf16[64,8,128]{2,0,1:T(8,128)(2,1)}), bf16[64,8,128]{2,0,1:T(8,128)(2,1)S(1)}, u32[]{:S(2)}, u32[]{:S(2)}) %all-to-all-start) | async-done | bytes 131104 | tf_op jit(solution)/shard_map/all_to_all | solution.py:147
  16.2 3.4 %all-to-all-start.2 = ((bf16[64,8,128]{2,0,1:T(8,128)(2,1)}), bf16[64,8,128]{2,0,1:T(8,128)(2,1)S(1)}, u32[]{:S(2)}, u32[]{:S(2)}) async-start(bf16[64,8,128]{2,0,1:T(8,128)(2,1)} %copy_bitcast_fusion.1), calls=%async_computation.2 | async-start | bytes 262144 | tf_op jit(solution)/shard_map/all_to_all | solution.py:150
  19.6 2.3 %copy.51 = bf16[8,8,8,1024]{3,2,0,1:T(8,128)(2,1)} copy(bf16[8,8,8,1024]{3,2,1,0:T(8,128)(2,1)} %bitcast.71) | data formatting | bytes 2097152 | tf_op jit(solution)/shard_map/reshape | solution.py:128
  21.9 5.0 %all-to-all-done.2 = bf16[64,8,128]{2,0,1:T(8,128)(2,1)S(1)} async-done(((bf16[64,8,128]{2,0,1:T(8,128)(2,1)}), bf16[64,8,128]{2,0,1:T(8,128)(2,1)S(1)}, u32[]{:S(2)}, u32[]{:S(2)}) %all-to-all-start.2) | async-done | bytes 131104 | tf_op jit(solution)/shard_map/all_to_all | solution.py:150
  26.9 3.6 %all-to-all-start.1 = ((bf16[64,8,1024]{2,0,1:T(8,128)(2,1)}), bf16[64,8,1024]{2,0,1:T(8,128)(2,1)S(1)}, u32[]{:S(2)}, u32[]{:S(2)}) async-start(bf16[64,8,1024]{2,0,1:T(8,128)(2,1)} %bitcast.66), calls=%async_computation.1 | async-start | bytes 2097152 | tf_op jit(solution)/shard_map/all_to_all | solution.py:127
  30.5 5.7 %gather_fusion = s32[1024]{0:T(1024)S(1)} fusion(s32[1024]{0:T(1024)} %param.12, s32[1024]{0:T(1024)S(1)} %broadcast_clamp_fusion), kind=kCustom, calls=%fused_computation | custom fusion | bytes 12288 | tf_op jit(solution)/shard_map/jit(_take)/gather | solution.py:175
  36.3 2.3 %gather_fusion.1 = s32[512]{0:T(512)S(1)} fusion(s32[1024]{0:T(1024)S(1)} %copy-done.1, s32[1024]{0:T(1024)S(1)} %pad_clamp_fusion), kind=kCustom, calls=%fused_computation.1 | custom fusion | bytes 6144 | tf_op jit(solution)/shard_map/jit(_take)/gather | solution.py:140
  38.8 6.8 %gather_fusion.2 = pred[1024]{0:T(1024)(128)(4,1)S(1)} fusion(pred[1024]{0:T(1024)(128)(4,1)S(1)} %fusion.24, s32[1024]{0:T(1024)S(1)} %broadcast_clamp_fusion), kind=kCustom, calls=%fused_computation.2 | custom fusion | bytes 6144 | tf_op jit(solution)/shard_map/jit(_take)/gather | solution.py:176
  48.1 2.0 %all_gather.6 = bf16[1024,128]{1,0:T(8,128)(2,1)S(1)} all-gather(bf16[512,128]{1,0:T(8,128)(2,1)S(1)} %bitcast.72), channel_id=1, replica_groups=mesh['groups'=2,'ulysses'=8,'seq'=2] {'seq'}, dimensions={0}, use_global_device_ids=true | all-gather | bytes 393216 | tf_op jit(solution)/shard_map/all_gather | solution.py:157
  50.1 2.1 %all_gather.7 = bf16[1024,128]{1,0:T(8,128)(2,1)} all-gather(bf16[512,128]{1,0:T(8,128)(2,1)S(1)} %bitcast.73), channel_id=1, replica_groups=mesh['groups'=2,'ulysses'=8,'seq'=2] {'seq'}, dimensions={0}, use_global_device_ids=true | all-gather | bytes 393216 | tf_op jit(solution)/shard_map/all_gather | solution.py:158
  52.2 1.9 %all-to-all-done.1 = bf16[64,8,1024]{2,0,1:T(8,128)(2,1)S(1)} async-done(((bf16[64,8,1024]{2,0,1:T(8,128)(2,1)}), bf16[64,8,1024]{2,0,1:T(8,128)(2,1)S(1)}, u32[]{:S(2)}, u32[]{:S(2)}) %all-to-all-start.1) | async-done | bytes 1048608 | tf_op jit(solution)/shard_map/all_to_all | solution.py:127
  55.2 31.6 %while.31 = (s32[]{:T(128)}, f32[512,8]{0,1:T(8,128)S(1)}, f32[512,8]{0,1:T(8,128)}, f32[512,8,128]{2,0,1:T(8,128)S(1)}, s32[1024]{0:T(1024)}, /*index=5*/s32[]{...) while((s32[]{:T(128)}, f32[512,8]{0,1:T(8,128)S(1)}, ...), condition=%wide.region_8.9_spmd.clone, body=%wide.region_2.8_spmd.clone.sunk | while | flops 1098925056 | bytes 33209420 | solution.py:96
  55.2 2.0 %fusion.67 = (s32[]{:T(128)}, s32[512]{0:T(512)}) fusion(s32[1024]{0:T(1024)} %get-tuple-element.768, s32[]{:T(128)} %select_n.391), kind=kLoop, calls=%fused_computation.117.clone.1 | loop fusion | flops 511 | bytes 4104 | tf_op jit(solution)/shard_map/while/body/eval_jaxpr/while/body/eval_jaxpr/reduce_min | solution.py:79
  61.5 9.5 %conditional.3 = ((f32[512,8]{0,1:T(8,128)S(1)}, f32[512,8]{0,1:T(8,128)}, f32[512,8,128]{2,0,1:T(8,128)S(1)})) conditional(s32[]{:T(128)} %convert_element_type.25, (f32[512,8]{0,1:T(8,128)S(1)}, f32[512,8]{0,1:T(8,128)}, f32[512,8,128]{2,0,1:T(8,128)S(1)}) %tuple.76, (s32[512]{0:T(512)}, s32[512]{0:T(512)}, s32[1024]{0:T(1024)}, s32[]{:T(128)}, ...), branch_computations={%region_4.4_spmd, %region_5.7_spmd.clone} | conditional | flops 1098922496 | bytes 33194124 | solution.py:78
  66.3 1.7 %fusion.3 = f32[512,8]{0,1:T(8,128)S(1)} fusion(f32[512,512,8]{1,0,2:T(8,128)S(1)} %get-tuple-element.622, f32[512,8]{0,1:T(8,128)S(1)} %max.5, pred[512,512]{0,1:T(8,128)(4,1)S(1)} %or_and_fusion), kind=kLoop, calls=%fused_computation.7 | loop fusion | flops 8384512 | bytes 8683520 | tf_op jit(solution)/shard_map/while/body/eval_jaxpr/while/body/eval_jaxpr/cond/branch_1_fun/reduce_sum | solution.py:35
  68.1 2.8 %multiply_add_fusion = f32[512,8,128]{2,0,1:T(8,128)S(1)} fusion(f32[512,8,128]{2,0,1:T(8,128)S(1)} %get-tuple-element.554, f32[512,512,8]{1,0,2:T(8,128)S(1)} %get-tuple-element.622, f32[512,8]{0,1:T(8,128)S(1)} %max.5, pred[512,512]{0,1:T(8,128)(4,1)S(1)} %or_and_fusion, f32[512,8]{0,1:T(8,128)S(1)} %get-tuple-element.618, ...), kind=kOutput, calls=%fused_computation.11 | convolution fusion | flops 546308096 | bytes 13008900 | tf_op jit(solution)/shard_map/while/body/eval_jaxpr/while/body/eval_jaxpr/cond/branch_1_fun/qhk,kd->qhd/dot_general | solution.py:36
  71.0 2.0 %fusion.67 = (s32[]{:T(128)}, s32[512]{0:T(512)}) fusion(s32[1024]{0:T(1024)} %get-tuple-element.768, s32[]{:T(128)} %select_n.391), kind=kLoop, calls=%fused_computation.117.clone.1 | loop fusion | flops 511 | bytes 4104 | tf_op jit(solution)/shard_map/while/body/eval_jaxpr/while/body/eval_jaxpr/reduce_min | solution.py:79
  77.3 9.5 %conditional.3 = ((f32[512,8]{0,1:T(8,128)S(1)}, f32[512,8]{0,1:T(8,128)}, f32[512,8,128]{2,0,1:T(8,128)S(1)})) conditional(s32[]{:T(128)} %convert_element_type.25, (f32[512,8]{0,1:T(8,128)S(1)}, f32[512,8]{0,1:T(8,128)}, f32[512,8,128]{2,0,1:T(8,128)S(1)}) %tuple.76, (s32[512]{0:T(512)}, s32[512]{0:T(512)}, s32[1024]{0:T(1024)}, s32[]{:T(128)}, ...), branch_computations={%region_4.4_spmd, %region_5.7_spmd.clone} | conditional | flops 1098922496 | bytes 33194124 | solution.py:78
  82.1 1.7 %fusion.3 = f32[512,8]{0,1:T(8,128)S(1)} fusion(f32[512,512,8]{1,0,2:T(8,128)S(1)} %get-tuple-element.622, f32[512,8]{0,1:T(8,128)S(1)} %max.5, pred[512,512]{0,1:T(8,128)(4,1)S(1)} %or_and_fusion), kind=kLoop, calls=%fused_computation.7 | loop fusion | flops 8384512 | bytes 8683520 | tf_op jit(solution)/shard_map/while/body/eval_jaxpr/while/body/eval_jaxpr/cond/branch_1_fun/reduce_sum | solution.py:35
  83.9 2.8 %multiply_add_fusion = f32[512,8,128]{2,0,1:T(8,128)S(1)} fusion(f32[512,8,128]{2,0,1:T(8,128)S(1)} %get-tuple-element.554, f32[512,512,8]{1,0,2:T(8,128)S(1)} %get-tuple-element.622, f32[512,8]{0,1:T(8,128)S(1)} %max.5, pred[512,512]{0,1:T(8,128)(4,1)S(1)} %or_and_fusion, f32[512,8]{0,1:T(8,128)S(1)} %get-tuple-element.618, ...), kind=kOutput, calls=%fused_computation.11 | convolution fusion | flops 546308096 | bytes 13008900 | tf_op jit(solution)/shard_map/while/body/eval_jaxpr/while/body/eval_jaxpr/cond/branch_1_fun/qhk,kd->qhd/dot_general | solution.py:36
  86.8 1.9 %copy.37 = f32[512,8,128]{0,2,1:T(8,128)} copy(f32[512,8,128]{2,0,1:T(8,128)S(1)} %get-tuple-element.428) | data formatting | bytes 4194304 | tf_op jit(solution)/shard_map/while/body/eval_jaxpr/while | solution.py:96
  88.7 1.9 %divide_convert_fusion = bf16[512,8,128]{0,2,1:T(8,128)(2,1)S(1)} fusion(f32[512,8,128]{0,2,1:T(8,128)} %copy.37, f32[512,8]{0,1:T(8,128)} %get-tuple-element.429), kind=kLoop, calls=%fused_computation.36 | loop fusion | flops 1048576 | bytes 3162112 | tf_op jit(solution)/shard_map/convert_element_type | solution.py:181
  93.8 29.9 %all_to_all.60 = bf16[8,2,32768]{2,1,0:T(2,128)(2,1)S(1)} all-to-all(bf16[8,2,32768]{2,1,0:T(2,128)(2,1)S(1)} %reshape.331), channel_id=1, replica_groups=mesh['groups'=2,'ulysses'=8,'seq'=2] {'ulysses'}, dimensions={0} | all-to-all | bytes 2097152 | tf_op jit(solution)/shard_map/all_to_all | solution.py:184
  (66 shorter events, 28.3 us)
Async XLA Ops:
  0.0 0.9 copy-start
  0.0 36.2 %copy-start.1 = (s32[1024]{0:T(1024)S(1)}, s32[1024]{0:T(1024)}, u32[]{:S(2)}) copy-start(s32[1024]{0:T(1024)} %param.12) | copy-start | bytes 12292
  0.9 37.7 %copy-start.5 = (s32[128]{0:T(128)S(1)}, s32[128]{0:T(128)}, u32[]{:S(2)}) copy-start(s32[128]{0:T(128)} %param.13) | copy-start | bytes 1540
  1.6 14.6 %all-to-all-start = ((bf16[64,8,128]{2,0,1:T(8,128)(2,1)}), bf16[64,8,128]{2,0,1:T(8,128)(2,1)S(1)}, u32[]{:S(2)}, u32[]{:S(2)}) async-start(bf16[64,8,128]{2,0,1:T(8,128)(2,1)} %copy_bitcast_fusion.2), calls=%async_computation | async-start | bytes 262144 | tf_op jit(solution)/shard_map/all_to_all | solution.py:147
  16.2 10.7 %all-to-all-start.2 = ((bf16[64,8,128]{2,0,1:T(8,128)(2,1)}), bf16[64,8,128]{2,0,1:T(8,128)(2,1)S(1)}, u32[]{:S(2)}, u32[]{:S(2)}) async-start(bf16[64,8,128]{2,0,1:T(8,128)(2,1)} %copy_bitcast_fusion.1), calls=%async_computation.2 | async-start | bytes 262144 | tf_op jit(solution)/shard_map/all_to_all | solution.py:150
  26.9 27.2 %all-to-all-start.1 = ((bf16[64,8,1024]{2,0,1:T(8,128)(2,1)}), bf16[64,8,1024]{2,0,1:T(8,128)(2,1)S(1)}, u32[]{:S(2)}, u32[]{:S(2)}) async-start(bf16[64,8,1024]{2,0,1:T(8,128)(2,1)} %bitcast.66), calls=%async_computation.1 | async-start | bytes 2097152 | tf_op jit(solution)/shard_map/all_to_all | solution.py:127
  64.8 3.3 %copy-start.2 = (f32[512,8]{0,1:T(8,128)S(1)}, f32[512,8]{0,1:T(8,128)}, u32[]{:S(2)}) copy-start(f32[512,8]{0,1:T(8,128)} %get-tuple-element.553) | copy-start | bytes 49156 | tf_op jit(solution)/shard_map/while/body/eval_jaxpr/while/body/eval_jaxpr/cond
  64.8 3.3 %copy-start.4 = (bf16[1024,128]{1,0:T(8,128)(2,1)S(1)}, bf16[1024,128]{1,0:T(8,128)(2,1)}, u32[]{:S(2)}) copy-start(bf16[1024,128]{1,0:T(8,128)(2,1)} %get-tuple-element.555) | copy-start | bytes 786436 | tf_op jit(solution)/shard_map/while/body/eval_jaxpr/while/body/eval_jaxpr/cond
  68.1 2.9 %copy-start.3 = (f32[512,8]{0,1:T(8,128)}, f32[512,8]{0,1:T(8,128)S(1)}, u32[]{:S(2)}) copy-start(f32[512,8]{0,1:T(8,128)S(1)} %get-tuple-element.726) | copy-start | bytes 49156 | tf_op jit(solution)/shard_map/while/body/eval_jaxpr/while/body/eval_jaxpr/cond
  80.6 3.3 %copy-start.2 = (f32[512,8]{0,1:T(8,128)S(1)}, f32[512,8]{0,1:T(8,128)}, u32[]{:S(2)}) copy-start(f32[512,8]{0,1:T(8,128)} %get-tuple-element.553) | copy-start | bytes 49156 | tf_op jit(solution)/shard_map/while/body/eval_jaxpr/while/body/eval_jaxpr/cond
  80.6 3.3 %copy-start.4 = (bf16[1024,128]{1,0:T(8,128)(2,1)S(1)}, bf16[1024,128]{1,0:T(8,128)(2,1)}, u32[]{:S(2)}) copy-start(bf16[1024,128]{1,0:T(8,128)(2,1)} %get-tuple-element.555) | copy-start | bytes 786436 | tf_op jit(solution)/shard_map/while/body/eval_jaxpr/while/body/eval_jaxpr/cond
  83.9 2.9 %copy-start.3 = (f32[512,8]{0,1:T(8,128)}, f32[512,8]{0,1:T(8,128)S(1)}, u32[]{:S(2)}) copy-start(f32[512,8]{0,1:T(8,128)S(1)} %get-tuple-element.726) | copy-start | bytes 49156 | tf_op jit(solution)/shard_map/while/body/eval_jaxpr/while/body/eval_jaxpr/cond
where the time goes:
time: 127 us; the launch traced here: 126 us
  local copies, waits for them, and re-layouts  34.1 us (27%)
  blocking collectives  34 us (27%)
  other arithmetic  19.5 us (15%)
  starting transfers between devices  14.2 us (11%)
  waiting for transfers between devices  12.6 us (10%)
  matrix products  8.7 us (7%)
  loops' own time  2.94 us (2%)
    all_to_all x1, blocking collectives, shards(): lax.all_to_all(result, 'ulysses', split_axis=0, concat_axis=1, tiled=True)  29.9 us
    all_to_all x1, starting transfers between devices, shards(): lax.all_to_all(spread(key_states, ulysses_count), 'ulysses', split_axis=1...  7.28 us
    gather x1, local copies, waits for them, and re-layouts, shards(): jnp.take(judged, key_place)  6.8 us
    all_to_all x1, waiting for transfers between devices, shards(): lax.all_to_all(spread(key_states, ulysses_count), 'ulysses', split_axis=1...  5.76 us
    gather x1, local copies, waits for them, and re-layouts, shards(): jnp.take(turn_ids, key_place)  5.72 us
    dot_general x2, matrix products, absorb(): jnp.einsum('qhk,kd->qhd', weights.astype(jnp.bfloat16), values_block, pre...  5.69 us
    unnamed x13, local copies, waits for them, and re-layouts  5.12 us
    all_to_all x1, waiting for transfers between devices, shards(): lax.all_to_all(spread(value_states, ulysses_count), 'ulysses', split_axis...  4.99 us
  transfers between devices with their start and end apart: 3, of which 3 were waited for; matrix products, arithmetic and copies ran while one was open for 17% of the time, Pallas kernels for 0%

commit v1 on v0

--- a/solution.py
+++ b/solution.py
@@ -6,6 +6,28 @@
 
 HEAD_DIM = 128
 floor_score = -1e30
+
+
+def in_blocks(x, dim, peers):
+    before, after = (x.shape[:dim], x.shape[dim + 1 :])
+    return jnp.moveaxis(x.reshape(*before, peers, -1, *after), dim, 0)
+
+
+def joined_along(parts, dim):
+    shape = list(parts.shape[1:])
+    shape[dim] *= parts.shape[0]
+    return jnp.moveaxis(parts, 0, dim).reshape(shape)
+
+
+def swapped_with_each(shard, axis, split_dim, concat_dim):
+    size, index = (lax.axis_size(axis), lax.axis_index(axis))
+    blocks = in_blocks(shard, split_dim, size)
+    outs = [blocks[index]]
+    for step in range(1, size):
+        sent = blocks[index ^ step]
+        outs.append(lax.ppermute(sent, axis, [(i, i ^ step) for i in range(size)]))
+    blocks = jnp.stack(outs)[index ^ jnp.arange(size)]
+    return joined_along(blocks, concat_dim)
 
 
 def absorb(
@@ -181,7 +203,7 @@
         .astype(jnp.bfloat16)
         .reshape(query_total, 1, heads_here * HEAD_DIM)
     )
-    returned = lax.all_to_all(result, "ulysses", split_axis=0, concat_axis=1, tiled=True)
+    returned = swapped_with_each(result, "ulysses", 0, 1)
     return returned.reshape(tokens_here, ulysses_count * heads_here * HEAD_DIM)
 
 

time: 127 us -> 119 us (0.937); the launches traced: 126 us -> 117 us
  blocking collectives: 34 us -> 4.1 us
  waiting for transfers between devices: 12.6 us -> 26.7 us
  starting transfers between devices: 14.2 us -> 25.7 us
  local copies, waits for them, and re-layouts: 34.1 us -> 30.9 us
  other arithmetic: 19.5 us -> 17.5 us
    all_to_all x1 -> x0, blocking collectives: 29.9 us -> none  [shards(): lax.all_to_all(result, 'ulysses', split_axis=0, concat_axis=1, tiled=True)]
    ppermute x0 -> x7, waiting for transfers between devices: none -> 14.1 us  [swapped_with_each(): outs.append(lax.ppermute(sent, axis, [(i, i ^ step) for i in range(size)]))]
    ppermute x0 -> x7, starting transfers between devices: none -> 11.5 us  [swapped_with_each(): outs.append(lax.ppermute(sent, axis, [(i, i ^ step) for i in range(size)]))]
    unnamed x13 -> x15, local copies, waits for them, and re-layouts: 5.12 us -> 2.44 us
    while x1 -> x0, local copies, waits for them, and re-layouts: 1.85 us -> none  [over_queries(): window = lax.fori_loop(0, key_count // key_step, over_keys, window)]
    reshape x1 -> x0, other arithmetic: 1.45 us -> none  [shards(): result = (running / totals[:, :, None]).astype(jnp.bfloat16).reshape(quer...]
  transfers between devices with their start and end apart: 3 -> 10, of which waited for: 3 -> 7; matrix products, arithmetic and copies ran while one was open for 17% -> 18% of each run, Pallas kernels for 0% -> 0%
where the time goes in v1:
time: 119 us; the launch traced here: 117 us
  local copies, waits for them, and re-layouts  30.9 us (26%)
  waiting for transfers between devices  26.7 us (22%)
  starting transfers between devices  25.7 us (22%)
  other arithmetic  17.5 us (15%)
  matrix products  8.69 us (7%)
  blocking collectives  4.1 us (3%)
  loops' own time  2.67 us (2%)
    ppermute x7, waiting for transfers between devices, swapped_with_each(): outs.append(lax.ppermute(sent, axis, [(i, i ^ step) for i in range(size)]))  14.1 us
    ppermute x7, starting transfers between devices, swapped_with_each(): outs.append(lax.ppermute(sent, axis, [(i, i ^ step) for i in range(size)]))  11.5 us
    all_to_all x1, starting transfers between devices, shards(): lax.all_to_all(spread(key_states, ulysses_count), 'ulysses', split_axis=1...  7.28 us
    gather x1, local copies, waits for them, and re-layouts, shards(): jnp.take(judged, key_place)  6.8 us
    all_to_all x1, waiting for transfers between devices, shards(): lax.all_to_all(spread(key_states, ulysses_count), 'ulysses', split_axis=1...  5.76 us
    gather x1, local copies, waits for them, and re-layouts, shards(): jnp.take(turn_ids, key_place)  5.72 us
    dot_general x2, matrix products, absorb(): jnp.einsum('qhk,kd->qhd', weights.astype(jnp.bfloat16), values_block, pre...  5.68 us
    all_to_all x1, waiting for transfers between devices, shards(): lax.all_to_all(spread(value_states, ulysses_count), 'ulysses', split_axis...  4.99 us
  transfers between devices with their start and end apart: 10, of which 7 were waited for; matrix products, arithmetic and copies ran while one was open for 18% of the time, Pallas kernels for 0%

profile of v1, /device:TPU:0, one launch (start us, length us, event | category | flops | bytes accessed | tf_op | source)
XLA Modules:
  0.0 116.6 jit_solution(6946670938973504655)
XLA Ops:
  1.6 7.3 %all-to-all-start = ((bf16[64,8,128]{2,0,1:T(8,128)(2,1)}), bf16[64,8,128]{2,0,1:T(8,128)(2,1)S(1)}, u32[]{:S(2)}, u32[]{:S(2)}) async-start(bf16[64,8,128]{2,0,1:T(8,128)(2,1)} %copy_bitcast_fusion.2), calls=%async_computation | async-start | bytes 262144 | tf_op jit(solution)/shard_map/all_to_all | solution.py:169
  10.5 5.8 %all-to-all-done = bf16[64,8,128]{2,0,1:T(8,128)(2,1)S(1)} async-done(((bf16[64,8,128]{2,0,1:T(8,128)(2,1)}), bf16[64,8,128]{2,0,1:T(8,128)(2,1)S(1)}, u32[]{:S(2)}, u32[]{:S(2)}) %all-to-all-start) | async-done | bytes 131104 | tf_op jit(solution)/shard_map/all_to_all | solution.py:169
  16.2 3.4 %all-to-all-start.2 = ((bf16[64,8,128]{2,0,1:T(8,128)(2,1)}), bf16[64,8,128]{2,0,1:T(8,128)(2,1)S(1)}, u32[]{:S(2)}, u32[]{:S(2)}) async-start(bf16[64,8,128]{2,0,1:T(8,128)(2,1)} %copy_bitcast_fusion.1), calls=%async_computation.2 | async-start | bytes 262144 | tf_op jit(solution)/shard_map/all_to_all | solution.py:172
  19.6 2.3 %copy.60 = bf16[8,8,8,1024]{3,2,0,1:T(8,128)(2,1)} copy(bf16[8,8,8,1024]{3,2,1,0:T(8,128)(2,1)} %bitcast.115) | data formatting | bytes 2097152 | tf_op jit(solution)/shard_map/reshape | solution.py:150
  21.9 5.0 %all-to-all-done.2 = bf16[64,8,128]{2,0,1:T(8,128)(2,1)S(1)} async-done(((bf16[64,8,128]{2,0,1:T(8,128)(2,1)}), bf16[64,8,128]{2,0,1:T(8,128)(2,1)S(1)}, u32[]{:S(2)}, u32[]{:S(2)}) %all-to-all-start.2) | async-done | bytes 131104 | tf_op jit(solution)/shard_map/all_to_all | solution.py:172
  26.9 3.6 %all-to-all-start.1 = ((bf16[64,8,1024]{2,0,1:T(8,128)(2,1)}), bf16[64,8,1024]{2,0,1:T(8,128)(2,1)S(1)}, u32[]{:S(2)}, u32[]{:S(2)}) async-start(bf16[64,8,1024]{2,0,1:T(8,128)(2,1)} %bitcast.110), calls=%async_computation.1 | async-start | bytes 2097152 | tf_op jit(solution)/shard_map/all_to_all | solution.py:149
  30.5 5.7 %gather_fusion = s32[1024]{0:T(1024)S(1)} fusion(s32[1024]{0:T(1024)} %param.12, s32[1024]{0:T(1024)S(1)} %broadcast_clamp_fusion), kind=kCustom, calls=%fused_computation | custom fusion | bytes 12288 | tf_op jit(solution)/shard_map/jit(_take)/gather | solution.py:197
  36.3 2.3 %gather_fusion.1 = s32[512]{0:T(512)S(1)} fusion(s32[1024]{0:T(1024)S(1)} %copy-done.1, s32[1024]{0:T(1024)S(1)} %pad_clamp_fusion.1), kind=kCustom, calls=%fused_computation.1 | custom fusion | bytes 6144 | tf_op jit(solution)/shard_map/jit(_take)/gather | solution.py:162
  38.8 6.8 %gather_fusion.2 = pred[1024]{0:T(1024)(128)(4,1)S(1)} fusion(pred[1024]{0:T(1024)(128)(4,1)S(1)} %fusion.24, s32[1024]{0:T(1024)S(1)} %broadcast_clamp_fusion), kind=kCustom, calls=%fused_computation.2 | custom fusion | bytes 6144 | tf_op jit(solution)/shard_map/jit(_take)/gather | solution.py:198
  48.1 2.0 %all_gather.6 = bf16[1024,128]{1,0:T(8,128)(2,1)S(1)} all-gather(bf16[512,128]{1,0:T(8,128)(2,1)S(1)} %bitcast.116), channel_id=1, replica_groups=mesh['groups'=2,'ulysses'=8,'seq'=2] {'seq'}, dimensions={0}, use_global_device_ids=true | all-gather | bytes 393216 | tf_op jit(solution)/shard_map/all_gather | solution.py:179
  50.1 2.1 %all_gather.7 = bf16[1024,128]{1,0:T(8,128)(2,1)} all-gather(bf16[512,128]{1,0:T(8,128)(2,1)S(1)} %bitcast.117), channel_id=1, replica_groups=mesh['groups'=2,'ulysses'=8,'seq'=2] {'seq'}, dimensions={0}, use_global_device_ids=true | all-gather | bytes 393216 | tf_op jit(solution)/shard_map/all_gather | solution.py:180
  55.2 31.2 %while.31 = (s32[]{:T(128)}, f32[512,8]{0,1:T(8,128)S(1)}, f32[512,8]{0,1:T(8,128)}, f32[512,8,128]{2,0,1:T(8,128)S(1)}, s32[1024]{0:T(1024)}, /*index=5*/s32[]{...) while((s32[]{:T(128)}, f32[512,8]{0,1:T(8,128)S(1)}, ...), condition=%wide.region_8.9_spmd.clone, body=%wide.region_2.8_spmd.clone.sunk | while | flops 1098925056 | bytes 33209420 | solution.py:118
  55.2 2.0 %fusion.68 = (s32[]{:T(128)}, s32[512]{0:T(512)}) fusion(s32[1024]{0:T(1024)} %get-tuple-element.763, s32[]{:T(128)} %select_n.437), kind=kLoop, calls=%fused_computation.136.clone.1 | loop fusion | flops 511 | bytes 4104 | tf_op jit(solution)/shard_map/while/body/eval_jaxpr/while/body/eval_jaxpr/reduce_min | solution.py:101
  61.3 9.5 %conditional.3 = ((f32[512,8]{0,1:T(8,128)S(1)}, f32[512,8]{0,1:T(8,128)}, f32[512,8,128]{2,0,1:T(8,128)S(1)})) conditional(s32[]{:T(128)} %convert_element_type.25, (f32[512,8]{0,1:T(8,128)S(1)}, f32[512,8]{0,1:T(8,128)}, f32[512,8,128]{2,0,1:T(8,128)S(1)}) %tuple.82, (s32[512]{0:T(512)}, s32[512]{0:T(512)}, s32[1024]{0:T(1024)}, s32[]{:T(128)}, ...), branch_computations={%region_4.4_spmd, %region_5.7_spmd.clone} | conditional | flops 1098922496 | bytes 33194124 | solution.py:100
  68.0 2.8 %multiply_add_fusion = f32[512,8,128]{2,0,1:T(8,128)S(1)} fusion(f32[512,8,128]{2,0,1:T(8,128)S(1)} %get-tuple-element.541, f32[512,512,8]{1,0,2:T(8,128)S(1)} %get-tuple-element.609, f32[512,8]{0,1:T(8,128)S(1)} %max.5, pred[512,512]{0,1:T(8,128)(4,1)S(1)} %or_and_fusion, f32[512,8]{0,1:T(8,128)S(1)} %get-tuple-element.605, ...), kind=kOutput, calls=%fused_computation.12 | convolution fusion | flops 546308096 | bytes 13008900 | tf_op jit(solution)/shard_map/while/body/eval_jaxpr/while/body/eval_jaxpr/cond/branch_1_fun/qhk,kd->qhd/dot_general | solution.py:58
  70.9 2.0 %fusion.68 = (s32[]{:T(128)}, s32[512]{0:T(512)}) fusion(s32[1024]{0:T(1024)} %get-tuple-element.763, s32[]{:T(128)} %select_n.437), kind=kLoop, calls=%fused_computation.136.clone.1 | loop fusion | flops 511 | bytes 4104 | tf_op jit(solution)/shard_map/while/body/eval_jaxpr/while/body/eval_jaxpr/reduce_min | solution.py:101
  76.9 9.5 %conditional.3 = ((f32[512,8]{0,1:T(8,128)S(1)}, f32[512,8]{0,1:T(8,128)}, f32[512,8,128]{2,0,1:T(8,128)S(1)})) conditional(s32[]{:T(128)} %convert_element_type.25, (f32[512,8]{0,1:T(8,128)S(1)}, f32[512,8]{0,1:T(8,128)}, f32[512,8,128]{2,0,1:T(8,128)S(1)}) %tuple.82, (s32[512]{0:T(512)}, s32[512]{0:T(512)}, s32[1024]{0:T(1024)}, s32[]{:T(128)}, ...), branch_computations={%region_4.4_spmd, %region_5.7_spmd.clone} | conditional | flops 1098922496 | bytes 33194124 | solution.py:100
  83.6 2.8 %multiply_add_fusion = f32[512,8,128]{2,0,1:T(8,128)S(1)} fusion(f32[512,8,128]{2,0,1:T(8,128)S(1)} %get-tuple-element.541, f32[512,512,8]{1,0,2:T(8,128)S(1)} %get-tuple-element.609, f32[512,8]{0,1:T(8,128)S(1)} %max.5, pred[512,512]{0,1:T(8,128)(4,1)S(1)} %or_and_fusion, f32[512,8]{0,1:T(8,128)S(1)} %get-tuple-element.605, ...), kind=kOutput, calls=%fused_computation.12 | convolution fusion | flops 546308096 | bytes 13008900 | tf_op jit(solution)/shard_map/while/body/eval_jaxpr/while/body/eval_jaxpr/cond/branch_1_fun/qhk,kd->qhd/dot_general | solution.py:58
  90.9 2.0 %collective-permute-start.2 = (bf16[64,1,1024]{2,0,1:T(8,128)(2,1)S(1)}, bf16[64,1,1024]{2,0,1:T(8,128)(2,1)S(1)}, u32[]{:S(2)}, u32[]{:S(2)}) collective-permute-start(bf16[64,1,1024]{2,0,1:T(8,128)(2,1)S(1)} %get-tuple-element.616), channel_id=1, source_target_pairs={{0,6},{2,4},{4,2},{6,0},{8,14},{10,12},{12,10},{14,8},{1,7},{3,5},... | collective-permute-start | bytes 393224 | tf_op jit(solution)/shard_map/ppermute | solution.py:28
  93.8 2.6 %collective-permute-start.4 = (bf16[64,1,1024]{2,0,1:T(8,128)(2,1)S(1)}, bf16[64,1,1024]{2,0,1:T(8,128)(2,1)S(1)}, u32[]{:S(2)}, u32[]{:S(2)}) collective-permute-start(bf16[64,1,1024]{2,0,1:T(8,128)(2,1)S(1)} %get-tuple-element.614), channel_id=1, source_target_pairs={{0,10},{2,8},{4,14},{6,12},{8,2},{10,0},{12,6},{14,4},{1,11},{3,9}... | collective-permute-start | bytes 393224 | tf_op jit(solution)/shard_map/ppermute | solution.py:28
  96.5 2.1 %collective-permute-start.5 = (bf16[64,1,1024]{2,0,1:T(8,128)(2,1)S(1)}, bf16[64,1,1024]{2,0,1:T(8,128)(2,1)S(1)}, u32[]{:S(2)}, u32[]{:S(2)}) collective-permute-start(bf16[64,1,1024]{2,0,1:T(8,128)(2,1)S(1)} %get-tuple-element.613), channel_id=1, source_target_pairs={{0,12},{2,14},{4,8},{6,10},{8,4},{10,6},{12,0},{14,2},{1,13},{3,15... | collective-permute-start | bytes 393224 | tf_op jit(solution)/shard_map/ppermute | solution.py:28
  98.6 2.2 %collective-permute-start.6 = (bf16[64,1,1024]{2,0,1:T(8,128)(2,1)S(1)}, bf16[64,1,1024]{2,0,1:T(8,128)(2,1)S(1)}, u32[]{:S(2)}, u32[]{:S(2)}) collective-permute-start(bf16[64,1,1024]{2,0,1:T(8,128)(2,1)S(1)} %get-tuple-element.612), channel_id=1, source_target_pairs={{0,14},{2,12},{4,10},{6,8},{8,6},{10,4},{12,2},{14,0},{1,15},{3,13... | collective-permute-start | bytes 393224 | tf_op jit(solution)/shard_map/ppermute | solution.py:28
  101.7 9.7 %collective-permute-done.3 = bf16[64,1,1024]{2,0,1:T(8,128)(2,1)S(1)} collective-permute-done((bf16[64,1,1024]{2,0,1:T(8,128)(2,1)S(1)}, bf16[64,1,1024]{2,0,1:T(8,128)(2,1)S(1)}, u32[]{:S(2)}, u32[]{:S(2)}) %collective-permute-start.3) | collective-permute-done | bytes 131104 | tf_op jit(solution)/shard_map/ppermute | solution.py:28
  111.4 3.5 %collective-permute-done.4 = bf16[64,1,1024]{2,0,1:T(8,128)(2,1)S(1)} collective-permute-done((bf16[64,1,1024]{2,0,1:T(8,128)(2,1)S(1)}, bf16[64,1,1024]{2,0,1:T(8,128)(2,1)S(1)}, u32[]{:S(2)}, u32[]{:S(2)}) %collective-permute-start.4) | collective-permute-done | bytes 131104 | tf_op jit(solution)/shard_map/ppermute | solution.py:28
  (85 shorter events, 35.8 us)
Async XLA Ops:
  0.0 0.9 copy-start
  0.0 36.3 %copy-start.1 = (s32[1024]{0:T(1024)S(1)}, s32[1024]{0:T(1024)}, u32[]{:S(2)}) copy-start(s32[1024]{0:T(1024)} %param.12) | copy-start | bytes 12292
  0.9 37.7 %copy-start.5 = (s32[128]{0:T(128)S(1)}, s32[128]{0:T(128)}, u32[]{:S(2)}) copy-start(s32[128]{0:T(128)} %param.13) | copy-start | bytes 1540
  1.6 14.6 %all-to-all-start = ((bf16[64,8,128]{2,0,1:T(8,128)(2,1)}), bf16[64,8,128]{2,0,1:T(8,128)(2,1)S(1)}, u32[]{:S(2)}, u32[]{:S(2)}) async-start(bf16[64,8,128]{2,0,1:T(8,128)(2,1)} %copy_bitcast_fusion.2), calls=%async_computation | async-start | bytes 262144 | tf_op jit(solution)/shard_map/all_to_all | solution.py:169
  16.2 10.7 %all-to-all-start.2 = ((bf16[64,8,128]{2,0,1:T(8,128)(2,1)}), bf16[64,8,128]{2,0,1:T(8,128)(2,1)S(1)}, u32[]{:S(2)}, u32[]{:S(2)}) async-start(bf16[64,8,128]{2,0,1:T(8,128)(2,1)} %copy_bitcast_fusion.1), calls=%async_computation.2 | async-start | bytes 262144 | tf_op jit(solution)/shard_map/all_to_all | solution.py:172
  26.9 27.2 %all-to-all-start.1 = ((bf16[64,8,1024]{2,0,1:T(8,128)(2,1)}), bf16[64,8,1024]{2,0,1:T(8,128)(2,1)S(1)}, u32[]{:S(2)}, u32[]{:S(2)}) async-start(bf16[64,8,1024]{2,0,1:T(8,128)(2,1)} %bitcast.110), calls=%async_computation.1 | async-start | bytes 2097152 | tf_op jit(solution)/shard_map/all_to_all | solution.py:149
  64.6 3.3 %copy-start.2 = (f32[512,8]{0,1:T(8,128)S(1)}, f32[512,8]{0,1:T(8,128)}, u32[]{:S(2)}) copy-start(f32[512,8]{0,1:T(8,128)} %get-tuple-element.540) | copy-start | bytes 49156 | tf_op jit(solution)/shard_map/while/body/eval_jaxpr/while/body/eval_jaxpr/cond
  64.6 3.3 %copy-start.4 = (bf16[1024,128]{1,0:T(8,128)(2,1)S(1)}, bf16[1024,128]{1,0:T(8,128)(2,1)}, u32[]{:S(2)}) copy-start(bf16[1024,128]{1,0:T(8,128)(2,1)} %get-tuple-element.542) | copy-start | bytes 786436 | tf_op jit(solution)/shard_map/while/body/eval_jaxpr/while/body/eval_jaxpr/cond
  67.9 2.9 %copy-start.3 = (f32[512,8]{0,1:T(8,128)}, f32[512,8]{0,1:T(8,128)S(1)}, u32[]{:S(2)}) copy-start(f32[512,8]{0,1:T(8,128)S(1)} %get-tuple-element.721) | copy-start | bytes 49156 | tf_op jit(solution)/shard_map/while/body/eval_jaxpr/while/body/eval_jaxpr/cond
  80.2 3.3 %copy-start.2 = (f32[512,8]{0,1:T(8,128)S(1)}, f32[512,8]{0,1:T(8,128)}, u32[]{:S(2)}) copy-start(f32[512,8]{0,1:T(8,128)} %get-tuple-element.540) | copy-start | bytes 49156 | tf_op jit(solution)/shard_map/while/body/eval_jaxpr/while/body/eval_jaxpr/cond
  80.2 3.3 %copy-start.4 = (bf16[1024,128]{1,0:T(8,128)(2,1)S(1)}, bf16[1024,128]{1,0:T(8,128)(2,1)}, u32[]{:S(2)}) copy-start(bf16[1024,128]{1,0:T(8,128)(2,1)} %get-tuple-element.542) | copy-start | bytes 786436 | tf_op jit(solution)/shard_map/while/body/eval_jaxpr/while/body/eval_jaxpr/cond
  83.6 2.9 %copy-start.3 = (f32[512,8]{0,1:T(8,128)}, f32[512,8]{0,1:T(8,128)S(1)}, u32[]{:S(2)}) copy-start(f32[512,8]{0,1:T(8,128)S(1)} %get-tuple-element.721) | copy-start | bytes 49156 | tf_op jit(solution)/shard_map/while/body/eval_jaxpr/while/body/eval_jaxpr/cond
  89.2 7.2 %collective-permute-start = (bf16[64,1,1024]{2,0,1:T(8,128)(2,1)S(1)}, bf16[64,1,1024]{2,0,1:T(8,128)(2,1)S(1)}, u32[]{:S(2)}, u32[]{:S(2)}) collective-permute-start(bf16[64,1,1024]{2,0,1:T(8,128)(2,1)S(1)} %get-tuple-element.618), channel_id=1, source_target_pairs={{0,2},{2,0},{4,6},{6,4},{8,10},{10,8},{12,14},{14,12},{1,3},{3,1},... | collective-permute-start | bytes 393224 | tf_op jit(solution)/shard_map/ppermute | solution.py:28
  90.5 8.1 %collective-permute-start.1 = (bf16[64,1,1024]{2,0,1:T(8,128)(2,1)S(1)}, bf16[64,1,1024]{2,0,1:T(8,128)(2,1)S(1)}, u32[]{:S(2)}, u32[]{:S(2)}) collective-permute-start(bf16[64,1,1024]{2,0,1:T(8,128)(2,1)S(1)} %get-tuple-element.617), channel_id=1, source_target_pairs={{0,4},{2,6},{4,0},{6,2},{8,12},{10,14},{12,8},{14,10},{1,5},{3,7},... | collective-permute-start | bytes 393224 | tf_op jit(solution)/shard_map/ppermute | solution.py:28
  90.9 10.8 %collective-permute-start.2 = (bf16[64,1,1024]{2,0,1:T(8,128)(2,1)S(1)}, bf16[64,1,1024]{2,0,1:T(8,128)(2,1)S(1)}, u32[]{:S(2)}, u32[]{:S(2)}) collective-permute-start(bf16[64,1,1024]{2,0,1:T(8,128)(2,1)S(1)} %get-tuple-element.616), channel_id=1, source_target_pairs={{0,6},{2,4},{4,2},{6,0},{8,14},{10,12},{12,10},{14,8},{1,7},{3,5},... | collective-permute-start | bytes 393224 | tf_op jit(solution)/shard_map/ppermute | solution.py:28
  92.8 18.5 %collective-permute-start.3 = (bf16[64,1,1024]{2,0,1:T(8,128)(2,1)S(1)}, bf16[64,1,1024]{2,0,1:T(8,128)(2,1)S(1)}, u32[]{:S(2)}, u32[]{:S(2)}) collective-permute-start(bf16[64,1,1024]{2,0,1:T(8,128)(2,1)S(1)} %get-tuple-element.615), channel_id=1, source_target_pairs={{0,8},{2,10},{4,12},{6,14},{8,0},{10,2},{12,4},{14,6},{1,9},{3,11}... | collective-permute-start | bytes 393224 | tf_op jit(solution)/shard_map/ppermute | solution.py:28
  93.8 21.1 %collective-permute-start.4 = (bf16[64,1,1024]{2,0,1:T(8,128)(2,1)S(1)}, bf16[64,1,1024]{2,0,1:T(8,128)(2,1)S(1)}, u32[]{:S(2)}, u32[]{:S(2)}) collective-permute-start(bf16[64,1,1024]{2,0,1:T(8,128)(2,1)S(1)} %get-tuple-element.614), channel_id=1, source_target_pairs={{0,10},{2,8},{4,14},{6,12},{8,2},{10,0},{12,6},{14,4},{1,11},{3,9}... | collective-permute-start | bytes 393224 | tf_op jit(solution)/shard_map/ppermute | solution.py:28
  96.5 18.4 %collective-permute-start.5 = (bf16[64,1,1024]{2,0,1:T(8,128)(2,1)S(1)}, bf16[64,1,1024]{2,0,1:T(8,128)(2,1)S(1)}, u32[]{:S(2)}, u32[]{:S(2)}) collective-permute-start(bf16[64,1,1024]{2,0,1:T(8,128)(2,1)S(1)} %get-tuple-element.613), channel_id=1, source_target_pairs={{0,12},{2,14},{4,8},{6,10},{8,4},{10,6},{12,0},{14,2},{1,13},{3,15... | collective-permute-start | bytes 393224 | tf_op jit(solution)/shard_map/ppermute | solution.py:28
  98.6 16.3 %collective-permute-start.6 = (bf16[64,1,1024]{2,0,1:T(8,128)(2,1)S(1)}, bf16[64,1,1024]{2,0,1:T(8,128)(2,1)S(1)}, u32[]{:S(2)}, u32[]{:S(2)}) collective-permute-start(bf16[64,1,1024]{2,0,1:T(8,128)(2,1)S(1)} %get-tuple-element.612), channel_id=1, source_target_pairs={{0,14},{2,12},{4,10},{6,8},{8,6},{10,4},{12,2},{14,0},{1,15},{3,13... | collective-permute-start | bytes 393224 | tf_op jit(solution)/shard_map/ppermute | solution.py:28
